TPU v7x, 256 devices: a whole 4x4x8 slice. The times are simulated.
256 devices in a mesh: wide: 32 (over z_hi, x, core), narrow: 8 (over z_lo, y).
Axes of the slice: x: 4, y: 4, z: 8 (z_hi: 4, z_lo: 2; z = z_hi * 2 + z_lo), core: 2. Of those that a mesh axis runs over, the one named last changes fastest.
Arguments:
- resid: bfloat16 [1024, 5120], P('wide'), may hold values from -6 to 6
- final_gain: float32 [5120], replicated, may hold values from 0.25 to 1.75
- unembed: bfloat16 [16384, 5120], P('narrow', 'wide'), may hold values from -12 to 12
- labels: int32 [1024, 4], replicated, may hold values from 0 to 16383
- layer_in: bfloat16 [1024, 5120], P('wide'), may hold values from -6 to 6
- gate_value: bfloat16 [1024, 13824], P('wide', 'narrow'), may hold values from -0.29882812 to 2
- down_weight: bfloat16 [13824, 5120], P('narrow', 'wide'), may hold values from -0.078125 to 0.078125
- basis_in: bfloat16 [5120, 5120], P('wide', 'narrow'), may hold values from -0.078125 to 0.078125
- basis_out: bfloat16 [13824, 13824], P('narrow', 'wide'), may hold values from -0.0546875 to 0.0546875
Outputs:
- corrected: float32 [13824, 5120], P('wide', 'narrow')
All inputs are finite; a program needn't handle non-finite values.
Results may differ from a plain program's by a relative error of at most 0.002.
The roundings to bfloat16 on the way count: a program that leaves them out, or rounds other values in their place, can miss the bound.
Values may be sent and summed in bfloat16 or wider, within the bound.
A program may use at most 128 MiB of HBM per device.

v0:
```python
import jax
import jax.numpy as jnp
from jax import lax
from jax.sharding import PartitionSpec as P

SEQ = 256
EXAMPLES = 4
EPSILON = 1e-05


def sent_to_all(value, axis):
    copies = jnp.broadcast_to(value, (lax.axis_size(axis), *value.shape))
    return lax.all_to_all(copies, axis, split_axis=0, concat_axis=0, tiled=True)


def of_everyone(value, axis):
    return sent_to_all(value, axis).sum(axis=0)


def taken_together(value, axis):
    return sent_to_all(value, axis).max(axis=0)


def contract_last(left, right):
    return lax.dot_general(
        left, right, (((1,), (1,)), ((), ())), preferred_element_type=jnp.float32
    )


def per_device(
    resid, final_gain, unembed, labels, layer_in, gate_value, down_weight, basis_in, basis_out
):
    wide_count = lax.axis_size("wide")
    wide_place = lax.axis_index("wide")
    narrow_place = lax.axis_index("narrow")
    local_tokens, width = resid.shape
    all_tokens, samples = labels.shape
    column_part = width // wide_count
    vocab_part = unembed.shape[0]
    hidden_part = down_weight.shape[0]
    grad_rows = local_tokens * samples
    resid_cols, inputs_cols = (
        lax.all_to_all(resid, "wide", split_axis=1, concat_axis=0, tiled=True),
        lax.all_to_all(layer_in, "wide", split_axis=1, concat_axis=0, tiled=True),
    )
    resid_float = resid_cols.astype(jnp.float32)
    gain_cols = lax.dynamic_slice_in_dim(final_gain, wide_place * column_part, column_part, 0)
    square_sums = of_everyone(jnp.sum(resid_float * resid_float, axis=1), "wide")
    inverse = lax.rsqrt(square_sums / width + EPSILON)
    normed = (resid_float * inverse[:, None] * gain_cols).astype(jnp.bfloat16)
    logits = lax.psum_scatter(
        contract_last(normed, unembed), "wide", scatter_dimension=0, tiled=True
    )
    largest = taken_together(jnp.max(logits, axis=1), "narrow")
    scaled = jnp.exp(logits - largest[:, None])
    totals = of_everyone(jnp.sum(scaled, axis=1), "narrow")
    probs = (scaled / totals[:, None]).astype(jnp.bfloat16)
    common = jnp.dot(
        lax.all_gather(probs, "wide", axis=0, tiled=True),
        unembed,
        preferred_element_type=jnp.float32,
    )
    shifted = labels - narrow_place * vocab_part
    inside = ((shifted >= 0) & (shifted < vocab_part)).astype(jnp.float32)
    picked = (
        jnp.take(unembed, jnp.clip(shifted, 0, vocab_part - 1), axis=0).astype(jnp.float32)
        * inside[:, :, None]
    )
    label_part = (common[:, None, :] - picked).reshape(all_tokens * samples, column_part)
    label_grads = lax.psum(label_part, "narrow")
    grads_local = lax.all_to_all(
        label_grads, "wide", split_axis=0, concat_axis=1, tiled=True
    ).reshape(local_tokens, samples, width)
    resid_local = resid.astype(jnp.float32)
    inverse_local = lax.rsqrt(jnp.mean(resid_local * resid_local, axis=1) + EPSILON)
    inner = jnp.sum(final_gain * grads_local * resid_local[:, None, :], axis=2)
    back = (
        inverse_local[:, None, None] * final_gain * grads_local
        - resid_local[:, None, :] * (inverse_local**3)[:, None, None] * inner[:, :, None] / width
    )
    back = back.astype(jnp.bfloat16).reshape(grad_rows, width)
    hidden_grads = contract_last(back, lax.all_gather(down_weight, "wide", axis=1, tiled=True))
    gated = (
        hidden_grads.reshape(local_tokens, samples, hidden_part)
        * gate_value.astype(jnp.float32)[:, None, :]
    )
    gated = gated.astype(jnp.bfloat16).reshape(grad_rows, hidden_part)
    rotated_part = jnp.dot(
        lax.all_gather(gated, "wide", axis=0, tiled=True),
        basis_out,
        preferred_element_type=jnp.float32,
    )
    rotated = lax.psum(rotated_part, "narrow").astype(jnp.bfloat16)
    inputs_part = jnp.dot(inputs_cols, basis_in, preferred_element_type=jnp.float32)
    inputs_rot = lax.psum(inputs_part, "wide").astype(jnp.bfloat16)
    rot_blocks = rotated.reshape(EXAMPLES, SEQ, samples, rotated.shape[1])
    input_blocks = inputs_rot.reshape(EXAMPLES, SEQ, inputs_rot.shape[1])
    blocks = jnp.einsum(
        "etsj,etd->esjd", rot_blocks, input_blocks, preferred_element_type=jnp.float32
    )
    return jnp.mean(blocks * blocks, axis=(0, 1))


def solution(mesh):
    in_specs = (
        P("wide", None),
        P(),
        P("narrow", "wide"),
        P(),
        P("wide", None),
        P("wide", "narrow"),
        P("narrow", "wide"),
        P("wide", "narrow"),
        P("narrow", "wide"),
    )
    out_specs = P("wide", "narrow")
    return jax.shard_map(
        per_device, mesh=mesh, in_specs=in_specs, out_specs=out_specs, check_vma=False
    )
```

profile of v0, /device:TPU:70, one launch (start us, length us, event | category | flops | bytes accessed | tf_op | source)
XLA Modules:
  0.0 968.3 jit_solution(15569779703708332936)
XLA Ops:
  8.6 26.2 %all_to_all.66 = bf16[32,32,160]{2,0,1:T(8,128)(2,1)S(1)} all-to-all(bf16[32,32,160]{2,0,1:T(8,128)(2,1)S(1)} %copy.52), channel_id=1, replica_groups=mesh['wide'=32,'narrow'=8] {'wide'}, dimensions={1} | all-to-all | bytes 655360 | tf_op jit(solution)/shard_map/all_to_all | solution.py:43
  35.8 6.7 all-to-all-start.1
  42.6 6.6 all-to-all-done.1
  49.6 4.5 fusion.13
  54.1 119.5 %reduce-scatter.2.cloned.1.call-done = f32[32,2048]{1,0:T(8,128)} async-done(((f32[1024,2048]{1,0:T(8,128)}), f32[32,2048]{1,0:T(8,128)}) %reduce-scatter.2.cloned.1.call-update) | async-done | bytes 262160 | tf_op jit(solution)/shard_map/reduce_scatter | solution.py:51
  174.7 10.3 %all_to_all.67 = f32[8,1,32]{2,1,0:T(1,128)S(1)} all-to-all(f32[8,1,32]{2,1,0:T(1,128)S(1)} %broadcast_in_dim.41), channel_id=1, replica_groups=mesh['wide'=32,'narrow'=8] {'narrow'}, dimensions={0} | all-to-all | bytes 2048 | tf_op jit(solution)/shard_map/all_to_all | solution.py:13
  186.2 8.5 all_to_all.68
  202.4 16.9 %gather_fusion = bf16[4096,160]{1,0:T(8,128)(2,1)} fusion(bf16[2048,160]{1,0:T(8,128)(2,1)S(1)} %copy.59, s32[4096]{0:T(1024)S(1)} %broadcast_clamp_fusion), kind=kCustom, calls=%fused_computation | custom fusion | bytes 2637824 | tf_op jit(solution)/shard_map/jit(_take)/gather | solution.py:66
  219.4 34.8 %all-gather.4.cloned.1.call-done = bf16[1024,2048]{1,0:T(8,128)(2,1)} async-done(((bf16[32,2048]{1,0:T(8,128)(2,1)}), bf16[1024,2048]{1,0:T(8,128)(2,1)}) %all-gather.4.cloned.1.call-update) | async-done | bytes 4194320 | tf_op jit(solution)/shard_map/all_gather | solution.py:59
  254.2 3.5 fusion.14
  257.6 2.6 sub.32
  260.3 5.3 sub.33
  265.5 7.0 multiply_subtract_fusion
  272.5 5.1 copy.61
  278.2 89.5 %all-reduce.4.cloned.1.call-done = f32[32,128,160]{1,2,0:T(8,128)} async-done(((f32[32,128,160]{1,2,0:T(8,128)}), f32[32,128,160]{1,2,0:T(8,128)}) %all-reduce.4.cloned.1.call-update) | async-done | bytes 2621456 | tf_op jit(solution)/shard_map/psum | solution.py:70
  367.7 9.0 all-to-all-start.4
  377.0 2.1 mul.153
  379.1 5.7 mul.154
  386.8 58.8 %all-to-all-done.4 = f32[32,128,160]{1,2,0:T(8,128)} async-done(((f32[32,128,160]{1,2,0:T(8,128)}), f32[32,128,160]{1,2,0:T(8,128)}, u32[]{:S(2)}, u32[]{:S(2)}) %all-to-all-start.4) | async-done | bytes 2621472 | tf_op jit(solution)/shard_map/all_to_all | solution.py:71
  445.7 5.1 copy.62
  450.8 4.5 multiply_reduce_fusion.1
  455.4 5.8 reshape.127
  461.2 3.5 subtract_convert_fusion
  464.8 70.3 %all-gather.6.cloned.1.call-done = bf16[1728,5120]{0,1:T(8,128)(2,1)} async-done(((bf16[1728,160]{0,1:T(8,128)(2,1)}), bf16[1728,5120]{0,1:T(8,128)(2,1)}) %all-gather.6.cloned.1.call-update) | async-done | bytes 17694736 | tf_op jit(solution)/shard_map/all_gather | solution.py:82
  535.1 9.0 fusion.6
  546.5 36.9 %all_to_all.69 = bf16[32,32,160]{2,0,1:T(8,128)(2,1)S(1)} all-to-all(bf16[32,32,160]{2,0,1:T(8,128)(2,1)S(1)} %copy.66), channel_id=1, replica_groups=mesh['wide'=32,'narrow'=8] {'wide'}, dimensions={1} | all-to-all | bytes 655360 | tf_op jit(solution)/shard_map/all_to_all | solution.py:44
  585.4 192.2 %all-reduce.6 = bf16[1024,640]{1,0:T(8,128)(2,1)S(1)} all-reduce(f32[1024,640]{1,0:T(8,128)} %fusion.16), channel_id=1, replica_groups=mesh['wide'=32,'narrow'=8] {'wide'}, use_global_device_ids=true, to_apply=%region_11.12 | all-reduce | flops 655360 | bytes 3932160 | tf_op jit(solution)/shard_map/psum | solution.py:95
  777.7 11.7 %fusion.15 = f32[4096,432]{0,1:T(8,128)} fusion(bf16[4096,1728]{1,0:T(8,128)(2,1)} %all-gather.8.cloned.1.call-done, bf16[1728,432]{0,1:T(8,128)(2,1)S(1)} %copy-done), kind=kOutput, calls=%fused_computation.31 | convolution fusion | flops 6115295232 | bytes 22726656 | tf_op jit(solution)/shard_map/dot_general | solution.py:88
  789.4 152.2 %all-reduce.5 = bf16[4096,432]{0,1:T(8,128)(2,1)} all-reduce(f32[4096,432]{0,1:T(8,128)} %fusion.15), channel_id=1, replica_groups=mesh['wide'=32,'narrow'=8] {'narrow'}, use_global_device_ids=true, to_apply=%region_10.11 | all-reduce | flops 1769472 | bytes 10616832 | tf_op jit(solution)/shard_map/psum | solution.py:93
  941.7 6.4 copy.65
  948.1 7.0 reshape.129
  955.0 5.6 multiply_reduce_fusion
  (65 shorter events, 21.8 us)
Async XLA Ops:
  6.5 771.1 %copy-start = (bf16[1728,432]{0,1:T(8,128)(2,1)S(1)}, bf16[1728,432]{0,1:T(8,128)(2,1)}, u32[]{:S(2)}) copy-start(bf16[1728,432]{0,1:T(8,128)(2,1)} %param.17) | copy-start | bytes 4478980
  6.5 36.0 %copy-start.6 = (f32[5120]{0:T(1024)S(1)}, f32[5120]{0:T(1024)}, u32[]{:S(2)}) copy-start(f32[5120]{0:T(1024)} %param.10) | copy-start | bytes 61444
  6.5 43.0 %copy-start.2 = (bf16[2048,160]{0,1:T(8,128)(2,1)S(1)}, bf16[2048,160]{0,1:T(8,128)(2,1)}, u32[]{:S(2)}) copy-start(bf16[2048,160]{0,1:T(8,128)(2,1)} %param.11) | copy-start | bytes 1966084
  35.8 13.5 %all-to-all-start.1 = ((f32[32,1,1024]{2,1,0:T(1,128)}), f32[32,1,1024]{2,1,0:T(1,128)S(1)}, u32[]{:S(2)}, u32[]{:S(2)}) async-start(f32[32,1,1024]{2,1,0:T(1,128)} %broadcast_in_dim.40), calls=%async_computation.1 | async-start | bytes 262144 | tf_op jit(solution)/shard_map/all_to_all | solution.py:13
  42.5 131.2 %reduce-scatter.2.cloned.1.call-start = ((), (), s32[]{:S(2)}) async-start(), calls=%async_computation.7 | async-start | bytes 8650752 | tf_op jit(solution)/shard_map/reduce_scatter | solution.py:51
  54.1 143.0 %copy-start.7 = (s32[1024,4]{0,1:T(4,128)S(1)}, s32[1024,4]{0,1:T(4,128)}, u32[]{:S(2)}) copy-start(s32[1024,4]{0,1:T(4,128)} %param.12) | copy-start | bytes 49156
  54.1 200.1 %all-gather.4.cloned.1.call-start = ((), (), s32[]{:S(2)}) async-start(), calls=%async_computation.8 | async-start | bytes 4325376 | tf_op jit(solution)/shard_map/all_gather | solution.py:59
  196.5 171.2 %all-reduce.4.cloned.1.call-start = ((), (), s32[]{:S(2)}) async-start(), calls=%async_computation.9 | async-start | bytes 5242880 | tf_op jit(solution)/shard_map/psum | solution.py:70
  277.7 257.5 %all-gather.6.cloned.1.call-start = ((), (), s32[]{:S(2)}) async-start(), calls=%async_computation.10 | async-start | bytes 18923520 | tf_op jit(solution)/shard_map/all_gather | solution.py:82
  278.2 98.8 %copy-start.1 = (bf16[32,5120]{1,0:T(8,128)(2,1)S(1)}, bf16[32,5120]{1,0:T(8,128)(2,1)}, u32[]{:S(2)}) copy-start(bf16[32,5120]{1,0:T(8,128)(2,1)} %param.9) | copy-start | bytes 983044
  367.7 77.9 %all-to-all-start.4 = ((f32[32,128,160]{1,2,0:T(8,128)}), f32[32,128,160]{1,2,0:T(8,128)}, u32[]{:S(2)}, u32[]{:S(2)}) async-start(f32[32,128,160]{1,2,0:T(8,128)} %all-reduce.4.cloned.1.call-done), calls=%async_computation.5 | async-start | bytes 5242880 | tf_op jit(solution)/shard_map/all_to_all | solution.py:71
  376.7 400.9 %all-gather.8.cloned.1.call-start = ((), (), s32[]{:S(2)}) async-start(), calls=%async_computation.11 | async-start | bytes 15138816 | tf_op jit(solution)/shard_map/all_gather | solution.py:89
  379.1 5.7 copy-start.5
  464.8 80.8 %copy-start.3 = (bf16[32,5120]{1,0:T(8,128)(2,1)S(1)}, bf16[32,5120]{1,0:T(8,128)(2,1)}, u32[]{:S(2)}) copy-start(bf16[32,5120]{1,0:T(8,128)(2,1)} %param.13) | copy-start | bytes 983044
  544.2 39.2 %copy-start.4 = (bf16[160,640]{1,0:T(8,128)(2,1)S(1)}, bf16[160,640]{1,0:T(8,128)(2,1)}, u32[]{:S(2)}) copy-start(bf16[160,640]{1,0:T(8,128)(2,1)} %param.16) | copy-start | bytes 614404
Sparse Core Ops, SparseCore 0:
  54.2 119.3 reduce-scatter.1
  196.6 57.4 all-gather.3
  277.8 89.9 all-reduce.3
  370.1 164.9 all-gather.5
  545.6 118.2 all-gather.7
where the time goes:
time: 970 us; the launch traced here: 968 us
  blocking collectives  426 us (44%)
  waiting for transfers between devices  380 us (39%)
  local copies, waits for them, and re-layouts  73.3 us (8%)
  matrix products  36.3 us (4%)
  other arithmetic  22.6 us (2%)
  starting transfers between devices  16 us (2%)
  between operations  13.4 us (1%)
    psum x1, blocking collectives, per_device(): inputs_rot = lax.psum(inputs_part, 'wide').astype(jnp.bfloat16)  192 us
    psum x1, blocking collectives, per_device(): rotated = lax.psum(rotated_part, 'narrow').astype(jnp.bfloat16)  152 us
    reduce_scatter x1, waiting for transfers between devices, per_device(): lax.psum_scatter(contract_last(normed, unembed), 'wide', scatter_dimensio...  120 us
    psum x1, waiting for transfers between devices, per_device(): label_grads = lax.psum(label_part, 'narrow')  89.5 us
    all_gather x1, waiting for transfers between devices, per_device(): lax.all_gather(down_weight, 'wide', axis=1, tiled=True)  70.3 us
    all_to_all x1, waiting for transfers between devices, per_device(): lax.all_to_all(label_grads, 'wide', split_axis=0, concat_axis=1, tiled=True)  58.8 us
    all_to_all x1, blocking collectives, per_device(): lax.all_to_all(layer_in, 'wide', split_axis=1, concat_axis=0, tiled=True)  36.9 us
    all_gather x1, waiting for transfers between devices, per_device(): lax.all_gather(probs, 'wide', axis=0, tiled=True)  34.8 us
  transfers between devices with their start and end apart: 7, of which 6 were waited for; matrix products, arithmetic and copies ran while one was open for 6% of the time, Pallas kernels for 0%

commit v1 on v0

--- a/solution.py
+++ b/solution.py
@@ -67,7 +67,7 @@
         * inside[:, :, None]
     )
     label_part = (common[:, None, :] - picked).reshape(all_tokens * samples, column_part)
-    label_grads = lax.psum(label_part, "narrow")
+    label_grads = jnp.sum(lax.all_gather(label_part, "narrow"), axis=0)
     grads_local = lax.all_to_all(
         label_grads, "wide", split_axis=0, concat_axis=1, tiled=True
     ).reshape(local_tokens, samples, width)

time: 970 us -> 1090 us (1.12)
  waiting for transfers between devices: 380 us -> 476 us
    all_gather x0 -> x1, waiting for transfers between devices: none -> 211 us  [per_device(): label_grads = jnp.sum(lax.all_gather(label_part, 'narrow'), axis=0)]
    psum x1 -> x0, waiting for transfers between devices: 89.5 us -> none  [per_device(): label_grads = lax.psum(label_part, 'narrow')]
    all_gather x1, waiting for transfers between devices: 70.3 us -> 21.7 us  [per_device(): lax.all_gather(down_weight, 'wide', axis=1, tiled=True)]
    all_to_all x1, waiting for transfers between devices: 58.8 us -> 81.7 us  [per_device(): lax.all_to_all(label_grads, 'wide', split_axis=0, concat_axis=1, tiled=True)]
  transfers between devices with their start and end apart: 7 -> 7, of which waited for: 6 -> 6; matrix products, arithmetic and copies ran while one was open for 6% -> 7% of each run, Pallas kernels for 0% -> 0%
where the time goes in v1:
time: 1090 us; the launch traced here: 1080 us
  waiting for transfers between devices  476 us (44%)
  blocking collectives  424 us (39%)
  local copies, waits for them, and re-layouts  83.5 us (8%)
  matrix products  36.4 us (3%)
  other arithmetic  31.3 us (3%)
  starting transfers between devices  16.2 us (1%)
  between operations  13.4 us (1%)
    all_gather x1, waiting for transfers between devices, per_device(): label_grads = jnp.sum(lax.all_gather(label_part, 'narrow'), axis=0)  211 us
    psum x1, blocking collectives, per_device(): inputs_rot = lax.psum(inputs_part, 'wide').astype(jnp.bfloat16)  201 us
    psum x1, blocking collectives, per_device(): rotated = lax.psum(rotated_part, 'narrow').astype(jnp.bfloat16)  146 us
    reduce_scatter x1, waiting for transfers between devices, per_device(): lax.psum_scatter(contract_last(normed, unembed), 'wide', scatter_dimensio...  120 us
    all_to_all x1, waiting for transfers between devices, per_device(): lax.all_to_all(label_grads, 'wide', split_axis=0, concat_axis=1, tiled=True)  81.7 us
    all_gather x1, waiting for transfers between devices, per_device(): lax.all_gather(probs, 'wide', axis=0, tiled=True)  34.8 us
    all_to_all x1, blocking collectives, per_device(): lax.all_to_all(layer_in, 'wide', split_axis=1, concat_axis=0, tiled=True)  33.1 us
    all_to_all x1, blocking collectives, per_device(): lax.all_to_all(resid, 'wide', split_axis=1, concat_axis=0, tiled=True)  26.2 us
  transfers between devices with their start and end apart: 7, of which 6 were waited for; matrix products, arithmetic and copies ran while one was open for 7% of the time, Pallas kernels for 0%

profile of v1, /device:TPU:70, one launch (start us, length us, event | category | flops | bytes accessed | tf_op | source)
XLA Modules:
  0.0 1081.0 jit_solution(15226141320428896597)
XLA Ops:
  8.6 26.2 %all_to_all.66 = bf16[32,32,160]{2,0,1:T(8,128)(2,1)S(1)} all-to-all(bf16[32,32,160]{2,0,1:T(8,128)(2,1)S(1)} %copy.84), channel_id=1, replica_groups=mesh['wide'=32,'narrow'=8] {'wide'}, dimensions={1} | all-to-all | bytes 655360 | tf_op jit(solution)/shard_map/all_to_all | solution.py:43
  35.8 6.7 all-to-all-start.1
  42.6 6.6 all-to-all-done.1
  49.6 4.5 fusion.13
  54.1 119.5 %reduce-scatter.2.cloned.1.call-done = f32[32,2048]{1,0:T(8,128)} async-done(((f32[1024,2048]{1,0:T(8,128)}), f32[32,2048]{1,0:T(8,128)}) %reduce-scatter.2.cloned.1.call-update) | async-done | bytes 262160 | tf_op jit(solution)/shard_map/reduce_scatter | solution.py:51
  174.7 10.3 all_to_all.67
  186.2 8.5 all_to_all.68
  202.4 16.9 %gather_fusion = bf16[4096,160]{1,0:T(8,128)(2,1)} fusion(bf16[2048,160]{1,0:T(8,128)(2,1)S(1)} %copy.91, s32[4096]{0:T(1024)S(1)} %broadcast_clamp_fusion), kind=kCustom, calls=%fused_computation | custom fusion | bytes 2637824 | tf_op jit(solution)/shard_map/jit(_take)/gather | solution.py:66
  219.4 34.8 %all-gather.5.cloned.1.call-done = bf16[1024,2048]{1,0:T(8,128)(2,1)} async-done(((bf16[32,2048]{1,0:T(8,128)(2,1)}), bf16[1024,2048]{1,0:T(8,128)(2,1)}) %all-gather.5.cloned.1.call-update) | async-done | bytes 4194320 | tf_op jit(solution)/shard_map/all_gather | solution.py:59
  254.2 3.5 fusion.14
  260.3 5.3 sub.39
  265.5 7.0 multiply_subtract_fusion
  272.5 5.1 copy.93
  278.2 211.0 %all-gather.7.cloned.1.call-done = f32[8,4096,160]{1,2,0:T(8,128)} async-done(((f32[1,4096,160]{1,2,0:T(8,128)}), f32[8,4096,160]{1,2,0:T(8,128)}) %all-gather.7.cloned.1.call-update) | async-done | bytes 20971536 | tf_op jit(solution)/shard_map/all_gather | solution.py:70
  489.2 9.5 reduce_sum.80
  498.6 4.9 copy.108
  503.5 5.3 copy.96
  508.8 9.2 all-to-all-start.4
  520.5 5.6 mul.160
  528.1 81.7 %all-to-all-done.4 = f32[32,128,160]{1,2,0:T(8,128)} async-done(((f32[32,128,160]{1,2,0:T(8,128)}), f32[32,128,160]{1,2,0:T(8,128)}, u32[]{:S(2)}, u32[]{:S(2)}) %all-to-all-start.4) | async-done | bytes 2621472 | tf_op jit(solution)/shard_map/all_to_all | solution.py:71
  609.8 5.1 copy.97
  614.9 4.5 multiply_reduce_fusion.1
  619.6 5.8 reshape.194
  628.2 21.7 %all-gather.9.cloned.1.call-done = bf16[1728,5120]{0,1:T(8,128)(2,1)} async-done(((bf16[1728,160]{0,1:T(8,128)(2,1)}), bf16[1728,5120]{0,1:T(8,128)(2,1)}) %all-gather.9.cloned.1.call-update) | async-done | bytes 17694736 | tf_op jit(solution)/shard_map/all_gather | solution.py:82
  649.8 9.0 fusion.6
  661.2 33.1 %all_to_all.69 = bf16[32,32,160]{2,0,1:T(8,128)(2,1)S(1)} all-to-all(bf16[32,32,160]{2,0,1:T(8,128)(2,1)S(1)} %copy.101), channel_id=1, replica_groups=mesh['wide'=32,'narrow'=8] {'wide'}, dimensions={1} | all-to-all | bytes 655360 | tf_op jit(solution)/shard_map/all_to_all | solution.py:44
  696.3 200.5 %all-reduce.3 = bf16[1024,640]{1,0:T(8,128)(2,1)S(1)} all-reduce(f32[1024,640]{1,0:T(8,128)} %fusion.16), channel_id=1, replica_groups=mesh['wide'=32,'narrow'=8] {'wide'}, use_global_device_ids=true, to_apply=%region_11.12 | all-reduce | flops 655360 | bytes 3932160 | tf_op jit(solution)/shard_map/psum | solution.py:95
  896.9 11.7 %fusion.15 = f32[4096,432]{0,1:T(8,128)} fusion(bf16[4096,1728]{1,0:T(8,128)(2,1)} %all-gather.11.cloned.1.call-done, bf16[1728,432]{0,1:T(8,128)(2,1)S(1)} %copy-done), kind=kOutput, calls=%fused_computation.32 | convolution fusion | flops 6115295232 | bytes 22726656 | tf_op jit(solution)/shard_map/dot_general | solution.py:88
  908.6 145.7 %all-reduce.2 = bf16[4096,432]{0,1:T(8,128)(2,1)} all-reduce(f32[4096,432]{0,1:T(8,128)} %fusion.15), channel_id=1, replica_groups=mesh['wide'=32,'narrow'=8] {'narrow'}, use_global_device_ids=true, to_apply=%region_10.11 | all-reduce | flops 1769472 | bytes 10616832 | tf_op jit(solution)/shard_map/psum | solution.py:93
  1054.4 6.4 copy.100
  1060.7 7.0 reshape.196
  1067.7 5.6 multiply_reduce_fusion
  (68 shorter events, 29.4 us)
Async XLA Ops:
  6.5 890.3 %copy-start = (bf16[1728,432]{0,1:T(8,128)(2,1)S(1)}, bf16[1728,432]{0,1:T(8,128)(2,1)}, u32[]{:S(2)}) copy-start(bf16[1728,432]{0,1:T(8,128)(2,1)} %param.17) | copy-start | bytes 4478980
  6.5 36.0 %copy-start.6 = (f32[5120]{0:T(1024)S(1)}, f32[5120]{0:T(1024)}, u32[]{:S(2)}) copy-start(f32[5120]{0:T(1024)} %param.10) | copy-start | bytes 61444
  6.5 43.0 %copy-start.2 = (bf16[2048,160]{0,1:T(8,128)(2,1)S(1)}, bf16[2048,160]{0,1:T(8,128)(2,1)}, u32[]{:S(2)}) copy-start(bf16[2048,160]{0,1:T(8,128)(2,1)} %param.11) | copy-start | bytes 1966084
  35.8 13.5 %all-to-all-start.1 = ((f32[32,1,1024]{2,1,0:T(1,128)}), f32[32,1,1024]{2,1,0:T(1,128)S(1)}, u32[]{:S(2)}, u32[]{:S(2)}) async-start(f32[32,1,1024]{2,1,0:T(1,128)} %broadcast_in_dim.40), calls=%async_computation.1 | async-start | bytes 262144 | tf_op jit(solution)/shard_map/all_to_all | solution.py:13
  42.5 131.2 %reduce-scatter.2.cloned.1.call-start = ((), (), s32[]{:S(2)}) async-start(), calls=%async_computation.7 | async-start | bytes 8650752 | tf_op jit(solution)/shard_map/reduce_scatter | solution.py:51
  54.1 143.0 %copy-start.7 = (s32[1024,4]{0,1:T(4,128)S(1)}, s32[1024,4]{0,1:T(4,128)}, u32[]{:S(2)}) copy-start(s32[1024,4]{0,1:T(4,128)} %param.12) | copy-start | bytes 49156
  54.1 200.1 %all-gather.5.cloned.1.call-start = ((), (), s32[]{:S(2)}) async-start(), calls=%async_computation.8 | async-start | bytes 4325376 | tf_op jit(solution)/shard_map/all_gather | solution.py:59
  196.5 292.7 %all-gather.7.cloned.1.call-start = ((), (), s32[]{:S(2)}) async-start(), calls=%async_computation.9 | async-start | bytes 23592960 | tf_op jit(solution)/shard_map/all_gather | solution.py:70
  277.6 372.2 %all-gather.9.cloned.1.call-start = ((), (), s32[]{:S(2)}) async-start(), calls=%async_computation.10 | async-start | bytes 18923520 | tf_op jit(solution)/shard_map/all_gather | solution.py:82
  508.8 9.5 copy-start.1
  508.8 101.0 %all-to-all-start.4 = ((f32[32,128,160]{1,2,0:T(8,128)}), f32[32,128,160]{1,2,0:T(8,128)}, u32[]{:S(2)}, u32[]{:S(2)}) async-start(f32[32,128,160]{1,2,0:T(8,128)} %copy.96), calls=%async_computation.5 | async-start | bytes 5242880 | tf_op jit(solution)/shard_map/all_to_all | solution.py:71
  518.0 378.9 %all-gather.11.cloned.1.call-start = ((), (), s32[]{:S(2)}) async-start(), calls=%async_computation.11 | async-start | bytes 15138816 | tf_op jit(solution)/shard_map/all_gather | solution.py:89
  520.5 5.6 copy-start.5
  628.1 32.1 %copy-start.3 = (bf16[32,5120]{1,0:T(8,128)(2,1)S(1)}, bf16[32,5120]{1,0:T(8,128)(2,1)}, u32[]{:S(2)}) copy-start(bf16[32,5120]{1,0:T(8,128)(2,1)} %param.13) | copy-start | bytes 983044
  658.9 35.4 %copy-start.4 = (bf16[160,640]{1,0:T(8,128)(2,1)S(1)}, bf16[160,640]{1,0:T(8,128)(2,1)}, u32[]{:S(2)}) copy-start(bf16[160,640]{1,0:T(8,128)(2,1)} %param.16) | copy-start | bytes 614404
Sparse Core Ops, SparseCore 0:
  54.2 119.3 reduce-scatter.1
  196.6 57.4 all-gather.4
  277.7 211.4 all-gather.6
  491.6 158.1 all-gather.8
  660.3 119.0 all-gather.10
